TPU v7x, 32 devices: a whole 2x2x4 slice. The times are simulated.
32 devices in a mesh: feat: 16 (over z, y, x), rows: 2 (over core).
Axes of the slice: x: 2, y: 2, z: 4, core: 2. Of those that a mesh axis runs over, the one named last changes fastest.
Arguments:
- grads: bfloat16 [16384], P(('rows', 'feat')), may hold values from -6 to 6
- hessians: bfloat16 [16384], P(('rows', 'feat')), may hold values from 0.019897461 to 0.25
- nodes: int32 [16384], P(('rows', 'feat')), may hold values from 0 to 15
- bins: int32 [512, 16384], P('feat', 'rows'), may hold values from 0 to 255
Outputs:
- histogram: float32 [2, 16, 512, 256], P(None, 'rows', 'feat')
- best_gain: float32 [16], P('rows')
All inputs are finite; a program needn't handle non-finite values.
Results may differ from a plain program's by a relative error of at most 0.0003.
Values may be sent and summed in bfloat16 or wider, within the bound.
A program may use at most 64 MiB of HBM per device.

v0:
```python
import jax
import jax.numpy as jnp
from jax import lax
from jax.sharding import PartitionSpec as P

BINS = 256
NODES = 16
reg_lambda = 1.0
block_rows = 512


def split_gain(hist):
    left_g = jnp.cumsum(hist[0], axis=-1)
    left_h = jnp.cumsum(hist[1], axis=-1)
    total_g = left_g[..., -1:]
    total_h = left_h[..., -1:]
    gain = left_g * left_g / (left_h + reg_lambda)
    gain = gain + (total_g - left_g) ** 2 / (total_h - left_h + reg_lambda)
    gain = gain - total_g * total_g / (total_h + reg_lambda)
    return jnp.max(gain, axis=(1, 2))


def make_panel(grads, hessians, nodes):
    node_ids = lax.broadcasted_iota(jnp.int32, (NODES, nodes.shape[0]), 0)
    node_hot = (nodes[None, :] == node_ids).astype(jnp.bfloat16)
    return jnp.concatenate([grads[None, :] * node_hot, hessians[None, :] * node_hot], axis=0)


def add_block(hist, bins_block, panel_block):
    count = panel_block.shape[1]
    bin_ids = lax.broadcasted_iota(jnp.int32, (1, BINS, 1), 1)
    one_hot = (bins_block[:, None, :] == bin_ids).astype(jnp.bfloat16).reshape(-1, count)
    return hist + lax.dot_general(
        panel_block, one_hot, (((1,), (1,)), ((), ())), preferred_element_type=jnp.float32
    )


def accumulate(hist, bins_part, panel_part):
    count = panel_part.shape[1]

    def step(which, carry):
        begin = which * block_rows
        bins_block = lax.dynamic_slice_in_dim(bins_part, begin, block_rows, 1)
        panel_block = lax.dynamic_slice_in_dim(panel_part, begin, block_rows, 1)
        return add_block(carry, bins_block, panel_block)

    return lax.fori_loop(0, count // block_rows, step, hist)


def local(grads, hessians, nodes, bins):
    feat_dev = bins.shape[0]
    empty = jnp.zeros((2 * NODES, feat_dev * BINS), jnp.float32)
    local_panel = make_panel(grads, hessians, nodes)
    hist = accumulate(empty, bins, lax.all_gather(local_panel, "feat", axis=1, tiled=True))
    hist = hist.reshape(2, NODES, feat_dev, BINS)
    share = NODES // lax.axis_size("rows")
    total = lax.psum(hist, "rows")
    mine = lax.dynamic_slice_in_dim(total, lax.axis_index("rows") * share, share, 1)
    best = lax.pmax(split_gain(mine), "feat")
    return (mine, best)


def solution(mesh):
    return jax.shard_map(
        local,
        mesh=mesh,
        in_specs=(P(("rows", "feat")), P(("rows", "feat")), P(("rows", "feat")), P("feat", "rows")),
        out_specs=(P(None, "rows", "feat", None), P("rows")),
        check_vma=False,
    )
```

profile of v0, /device:TPU:0, one launch (start us, length us, event | category | flops | bytes accessed | tf_op | source)
XLA Modules:
  0.0 288.1 jit_solution(18204161635696154360)
XLA Ops:
  7.2 0.7 fusion.4
  7.9 45.3 %all_gather.3 = bf16[32,8192]{1,0:T(8,128)(2,1)S(1)} all-gather(bf16[32,512]{1,0:T(8,128)(2,1)S(1)} %pad_maximum_fusion), channel_id=1, replica_groups=mesh['feat'=16,'rows'=2] {'feat'}, dimensions={1}, use_global_device_ids=true | all-gather | bytes 557056 | tf_op jit(solution)/shard_map/all_gather | solution.py:54
  53.3 155.4 %while.14 = (s32[]{:T(128)}, f32[32,8192]{1,0:T(8,128)S(1)}, bf16[32,8192]{1,0:T(8,128)(2,1)S(1)}, s32[32,8192]{1,0:T(8,128)}, s32[]{:T(128)}, /*index=5*/s32[]{:T(128)}, s32[]{:T(128)}, s32[]{:T(128)}) while((s32[]{:T(128)}, f32[32,8192]{1,0:T(8,128)S(1)}, bf16[32,8192]{1,0:T(8,128)(2,1)S(1)}, s32[32,8192]{1,0:T(8,128)}, ...), condition=%wide.region_1.0_spmd.clone, body=%wide.region_0.0_spmd.clone.sunk | while | flops 273154048 | bytes 10846365 | solution.py:47
  53.3 0.9 constant_dynamic-slice_fusion.5
  54.2 4.0 %bitcast_compare_fusion.2 = pred[8192,512]{1,0:T(32,128)(4,1)} fusion(s32[8192]{0:T(1024)S(1)} %bitcast.39, s32[32,512]{1,0:T(8,128)S(1)} %constant_dynamic-slice_fusion.5), kind=kLoop, calls=%fused_computation.clone.1 | loop fusion | flops 4194304 | bytes 4292608 | tf_op jit(solution)/shard_map/while/body/eval_jaxpr/eq | solution.py:32
  58.1 4.8 %convolution_add_fusion.2 = f32[32,8192]{1,0:T(8,128)S(1)} fusion(pred[8192,512]{1,0:T(32,128)(4,1)} %bitcast_compare_fusion.2, f32[32,8192]{1,0:T(8,128)S(1)} %get-tuple-element.148, pred[]{:T(512)S(6)} %compare.3, bf16[32,8192]{1,0:T(8,128)(2,1)S(1)} %get-tuple-element.157, s32[]{:T(128)S(6)} %select_n.14), kind=kOutput, calls=%fused_computation.1.clone.1 | convolution fusion | flops 268959744 | bytes 6324229 | tf_op jit(solution)/shard_map/while/body/eval_jaxpr/dot_general | solution.py:33
  63.0 0.9 constant_dynamic-slice_fusion.5
  63.9 4.0 %bitcast_compare_fusion.2 = pred[8192,512]{1,0:T(32,128)(4,1)} fusion(s32[8192]{0:T(1024)S(1)} %bitcast.39, s32[32,512]{1,0:T(8,128)S(1)} %constant_dynamic-slice_fusion.5), kind=kLoop, calls=%fused_computation.clone.1 | loop fusion | flops 4194304 | bytes 4292608 | tf_op jit(solution)/shard_map/while/body/eval_jaxpr/eq | solution.py:32
  67.9 4.8 %convolution_add_fusion.2 = f32[32,8192]{1,0:T(8,128)S(1)} fusion(pred[8192,512]{1,0:T(32,128)(4,1)} %bitcast_compare_fusion.2, f32[32,8192]{1,0:T(8,128)S(1)} %get-tuple-element.148, pred[]{:T(512)S(6)} %compare.3, bf16[32,8192]{1,0:T(8,128)(2,1)S(1)} %get-tuple-element.157, s32[]{:T(128)S(6)} %select_n.14), kind=kOutput, calls=%fused_computation.1.clone.1 | convolution fusion | flops 268959744 | bytes 6324229 | tf_op jit(solution)/shard_map/while/body/eval_jaxpr/dot_general | solution.py:33
  72.7 0.9 constant_dynamic-slice_fusion.5
  73.6 4.0 %bitcast_compare_fusion.2 = pred[8192,512]{1,0:T(32,128)(4,1)} fusion(s32[8192]{0:T(1024)S(1)} %bitcast.39, s32[32,512]{1,0:T(8,128)S(1)} %constant_dynamic-slice_fusion.5), kind=kLoop, calls=%fused_computation.clone.1 | loop fusion | flops 4194304 | bytes 4292608 | tf_op jit(solution)/shard_map/while/body/eval_jaxpr/eq | solution.py:32
  77.6 4.8 %convolution_add_fusion.2 = f32[32,8192]{1,0:T(8,128)S(1)} fusion(pred[8192,512]{1,0:T(32,128)(4,1)} %bitcast_compare_fusion.2, f32[32,8192]{1,0:T(8,128)S(1)} %get-tuple-element.148, pred[]{:T(512)S(6)} %compare.3, bf16[32,8192]{1,0:T(8,128)(2,1)S(1)} %get-tuple-element.157, s32[]{:T(128)S(6)} %select_n.14), kind=kOutput, calls=%fused_computation.1.clone.1 | convolution fusion | flops 268959744 | bytes 6324229 | tf_op jit(solution)/shard_map/while/body/eval_jaxpr/dot_general | solution.py:33
  82.4 0.9 constant_dynamic-slice_fusion.5
  83.3 4.0 %bitcast_compare_fusion.2 = pred[8192,512]{1,0:T(32,128)(4,1)} fusion(s32[8192]{0:T(1024)S(1)} %bitcast.39, s32[32,512]{1,0:T(8,128)S(1)} %constant_dynamic-slice_fusion.5), kind=kLoop, calls=%fused_computation.clone.1 | loop fusion | flops 4194304 | bytes 4292608 | tf_op jit(solution)/shard_map/while/body/eval_jaxpr/eq | solution.py:32
  87.3 4.8 %convolution_add_fusion.2 = f32[32,8192]{1,0:T(8,128)S(1)} fusion(pred[8192,512]{1,0:T(32,128)(4,1)} %bitcast_compare_fusion.2, f32[32,8192]{1,0:T(8,128)S(1)} %get-tuple-element.148, pred[]{:T(512)S(6)} %compare.3, bf16[32,8192]{1,0:T(8,128)(2,1)S(1)} %get-tuple-element.157, s32[]{:T(128)S(6)} %select_n.14), kind=kOutput, calls=%fused_computation.1.clone.1 | convolution fusion | flops 268959744 | bytes 6324229 | tf_op jit(solution)/shard_map/while/body/eval_jaxpr/dot_general | solution.py:33
  92.2 0.9 constant_dynamic-slice_fusion.5
  93.0 4.0 %bitcast_compare_fusion.2 = pred[8192,512]{1,0:T(32,128)(4,1)} fusion(s32[8192]{0:T(1024)S(1)} %bitcast.39, s32[32,512]{1,0:T(8,128)S(1)} %constant_dynamic-slice_fusion.5), kind=kLoop, calls=%fused_computation.clone.1 | loop fusion | flops 4194304 | bytes 4292608 | tf_op jit(solution)/shard_map/while/body/eval_jaxpr/eq | solution.py:32
  97.0 4.8 %convolution_add_fusion.2 = f32[32,8192]{1,0:T(8,128)S(1)} fusion(pred[8192,512]{1,0:T(32,128)(4,1)} %bitcast_compare_fusion.2, f32[32,8192]{1,0:T(8,128)S(1)} %get-tuple-element.148, pred[]{:T(512)S(6)} %compare.3, bf16[32,8192]{1,0:T(8,128)(2,1)S(1)} %get-tuple-element.157, s32[]{:T(128)S(6)} %select_n.14), kind=kOutput, calls=%fused_computation.1.clone.1 | convolution fusion | flops 268959744 | bytes 6324229 | tf_op jit(solution)/shard_map/while/body/eval_jaxpr/dot_general | solution.py:33
  101.9 0.9 constant_dynamic-slice_fusion.5
  102.7 4.0 %bitcast_compare_fusion.2 = pred[8192,512]{1,0:T(32,128)(4,1)} fusion(s32[8192]{0:T(1024)S(1)} %bitcast.39, s32[32,512]{1,0:T(8,128)S(1)} %constant_dynamic-slice_fusion.5), kind=kLoop, calls=%fused_computation.clone.1 | loop fusion | flops 4194304 | bytes 4292608 | tf_op jit(solution)/shard_map/while/body/eval_jaxpr/eq | solution.py:32
  106.7 4.8 %convolution_add_fusion.2 = f32[32,8192]{1,0:T(8,128)S(1)} fusion(pred[8192,512]{1,0:T(32,128)(4,1)} %bitcast_compare_fusion.2, f32[32,8192]{1,0:T(8,128)S(1)} %get-tuple-element.148, pred[]{:T(512)S(6)} %compare.3, bf16[32,8192]{1,0:T(8,128)(2,1)S(1)} %get-tuple-element.157, s32[]{:T(128)S(6)} %select_n.14), kind=kOutput, calls=%fused_computation.1.clone.1 | convolution fusion | flops 268959744 | bytes 6324229 | tf_op jit(solution)/shard_map/while/body/eval_jaxpr/dot_general | solution.py:33
  111.6 0.9 constant_dynamic-slice_fusion.5
  112.4 4.0 %bitcast_compare_fusion.2 = pred[8192,512]{1,0:T(32,128)(4,1)} fusion(s32[8192]{0:T(1024)S(1)} %bitcast.39, s32[32,512]{1,0:T(8,128)S(1)} %constant_dynamic-slice_fusion.5), kind=kLoop, calls=%fused_computation.clone.1 | loop fusion | flops 4194304 | bytes 4292608 | tf_op jit(solution)/shard_map/while/body/eval_jaxpr/eq | solution.py:32
  116.4 4.8 %convolution_add_fusion.2 = f32[32,8192]{1,0:T(8,128)S(1)} fusion(pred[8192,512]{1,0:T(32,128)(4,1)} %bitcast_compare_fusion.2, f32[32,8192]{1,0:T(8,128)S(1)} %get-tuple-element.148, pred[]{:T(512)S(6)} %compare.3, bf16[32,8192]{1,0:T(8,128)(2,1)S(1)} %get-tuple-element.157, s32[]{:T(128)S(6)} %select_n.14), kind=kOutput, calls=%fused_computation.1.clone.1 | convolution fusion | flops 268959744 | bytes 6324229 | tf_op jit(solution)/shard_map/while/body/eval_jaxpr/dot_general | solution.py:33
  121.3 0.9 constant_dynamic-slice_fusion.5
  122.1 4.0 %bitcast_compare_fusion.2 = pred[8192,512]{1,0:T(32,128)(4,1)} fusion(s32[8192]{0:T(1024)S(1)} %bitcast.39, s32[32,512]{1,0:T(8,128)S(1)} %constant_dynamic-slice_fusion.5), kind=kLoop, calls=%fused_computation.clone.1 | loop fusion | flops 4194304 | bytes 4292608 | tf_op jit(solution)/shard_map/while/body/eval_jaxpr/eq | solution.py:32
  126.1 4.8 %convolution_add_fusion.2 = f32[32,8192]{1,0:T(8,128)S(1)} fusion(pred[8192,512]{1,0:T(32,128)(4,1)} %bitcast_compare_fusion.2, f32[32,8192]{1,0:T(8,128)S(1)} %get-tuple-element.148, pred[]{:T(512)S(6)} %compare.3, bf16[32,8192]{1,0:T(8,128)(2,1)S(1)} %get-tuple-element.157, s32[]{:T(128)S(6)} %select_n.14), kind=kOutput, calls=%fused_computation.1.clone.1 | convolution fusion | flops 268959744 | bytes 6324229 | tf_op jit(solution)/shard_map/while/body/eval_jaxpr/dot_general | solution.py:33
  131.0 0.9 constant_dynamic-slice_fusion.5
  131.9 4.0 %bitcast_compare_fusion.2 = pred[8192,512]{1,0:T(32,128)(4,1)} fusion(s32[8192]{0:T(1024)S(1)} %bitcast.39, s32[32,512]{1,0:T(8,128)S(1)} %constant_dynamic-slice_fusion.5), kind=kLoop, calls=%fused_computation.clone.1 | loop fusion | flops 4194304 | bytes 4292608 | tf_op jit(solution)/shard_map/while/body/eval_jaxpr/eq | solution.py:32
  135.8 4.8 %convolution_add_fusion.2 = f32[32,8192]{1,0:T(8,128)S(1)} fusion(pred[8192,512]{1,0:T(32,128)(4,1)} %bitcast_compare_fusion.2, f32[32,8192]{1,0:T(8,128)S(1)} %get-tuple-element.148, pred[]{:T(512)S(6)} %compare.3, bf16[32,8192]{1,0:T(8,128)(2,1)S(1)} %get-tuple-element.157, s32[]{:T(128)S(6)} %select_n.14), kind=kOutput, calls=%fused_computation.1.clone.1 | convolution fusion | flops 268959744 | bytes 6324229 | tf_op jit(solution)/shard_map/while/body/eval_jaxpr/dot_general | solution.py:33
  140.7 0.9 constant_dynamic-slice_fusion.5
  141.6 4.0 %bitcast_compare_fusion.2 = pred[8192,512]{1,0:T(32,128)(4,1)} fusion(s32[8192]{0:T(1024)S(1)} %bitcast.39, s32[32,512]{1,0:T(8,128)S(1)} %constant_dynamic-slice_fusion.5), kind=kLoop, calls=%fused_computation.clone.1 | loop fusion | flops 4194304 | bytes 4292608 | tf_op jit(solution)/shard_map/while/body/eval_jaxpr/eq | solution.py:32
  145.6 4.8 %convolution_add_fusion.2 = f32[32,8192]{1,0:T(8,128)S(1)} fusion(pred[8192,512]{1,0:T(32,128)(4,1)} %bitcast_compare_fusion.2, f32[32,8192]{1,0:T(8,128)S(1)} %get-tuple-element.148, pred[]{:T(512)S(6)} %compare.3, bf16[32,8192]{1,0:T(8,128)(2,1)S(1)} %get-tuple-element.157, s32[]{:T(128)S(6)} %select_n.14), kind=kOutput, calls=%fused_computation.1.clone.1 | convolution fusion | flops 268959744 | bytes 6324229 | tf_op jit(solution)/shard_map/while/body/eval_jaxpr/dot_general | solution.py:33
  150.4 0.9 constant_dynamic-slice_fusion.5
  151.3 4.0 %bitcast_compare_fusion.2 = pred[8192,512]{1,0:T(32,128)(4,1)} fusion(s32[8192]{0:T(1024)S(1)} %bitcast.39, s32[32,512]{1,0:T(8,128)S(1)} %constant_dynamic-slice_fusion.5), kind=kLoop, calls=%fused_computation.clone.1 | loop fusion | flops 4194304 | bytes 4292608 | tf_op jit(solution)/shard_map/while/body/eval_jaxpr/eq | solution.py:32
  155.3 4.8 %convolution_add_fusion.2 = f32[32,8192]{1,0:T(8,128)S(1)} fusion(pred[8192,512]{1,0:T(32,128)(4,1)} %bitcast_compare_fusion.2, f32[32,8192]{1,0:T(8,128)S(1)} %get-tuple-element.148, pred[]{:T(512)S(6)} %compare.3, bf16[32,8192]{1,0:T(8,128)(2,1)S(1)} %get-tuple-element.157, s32[]{:T(128)S(6)} %select_n.14), kind=kOutput, calls=%fused_computation.1.clone.1 | convolution fusion | flops 268959744 | bytes 6324229 | tf_op jit(solution)/shard_map/while/body/eval_jaxpr/dot_general | solution.py:33
  160.1 0.9 constant_dynamic-slice_fusion.5
  161.0 4.0 %bitcast_compare_fusion.2 = pred[8192,512]{1,0:T(32,128)(4,1)} fusion(s32[8192]{0:T(1024)S(1)} %bitcast.39, s32[32,512]{1,0:T(8,128)S(1)} %constant_dynamic-slice_fusion.5), kind=kLoop, calls=%fused_computation.clone.1 | loop fusion | flops 4194304 | bytes 4292608 | tf_op jit(solution)/shard_map/while/body/eval_jaxpr/eq | solution.py:32
  165.0 4.8 %convolution_add_fusion.2 = f32[32,8192]{1,0:T(8,128)S(1)} fusion(pred[8192,512]{1,0:T(32,128)(4,1)} %bitcast_compare_fusion.2, f32[32,8192]{1,0:T(8,128)S(1)} %get-tuple-element.148, pred[]{:T(512)S(6)} %compare.3, bf16[32,8192]{1,0:T(8,128)(2,1)S(1)} %get-tuple-element.157, s32[]{:T(128)S(6)} %select_n.14), kind=kOutput, calls=%fused_computation.1.clone.1 | convolution fusion | flops 268959744 | bytes 6324229 | tf_op jit(solution)/shard_map/while/body/eval_jaxpr/dot_general | solution.py:33
  169.9 0.9 constant_dynamic-slice_fusion.5
  170.7 4.0 %bitcast_compare_fusion.2 = pred[8192,512]{1,0:T(32,128)(4,1)} fusion(s32[8192]{0:T(1024)S(1)} %bitcast.39, s32[32,512]{1,0:T(8,128)S(1)} %constant_dynamic-slice_fusion.5), kind=kLoop, calls=%fused_computation.clone.1 | loop fusion | flops 4194304 | bytes 4292608 | tf_op jit(solution)/shard_map/while/body/eval_jaxpr/eq | solution.py:32
  174.7 4.8 %convolution_add_fusion.2 = f32[32,8192]{1,0:T(8,128)S(1)} fusion(pred[8192,512]{1,0:T(32,128)(4,1)} %bitcast_compare_fusion.2, f32[32,8192]{1,0:T(8,128)S(1)} %get-tuple-element.148, pred[]{:T(512)S(6)} %compare.3, bf16[32,8192]{1,0:T(8,128)(2,1)S(1)} %get-tuple-element.157, s32[]{:T(128)S(6)} %select_n.14), kind=kOutput, calls=%fused_computation.1.clone.1 | convolution fusion | flops 268959744 | bytes 6324229 | tf_op jit(solution)/shard_map/while/body/eval_jaxpr/dot_general | solution.py:33
  179.6 0.9 constant_dynamic-slice_fusion.5
  180.4 4.0 %bitcast_compare_fusion.2 = pred[8192,512]{1,0:T(32,128)(4,1)} fusion(s32[8192]{0:T(1024)S(1)} %bitcast.39, s32[32,512]{1,0:T(8,128)S(1)} %constant_dynamic-slice_fusion.5), kind=kLoop, calls=%fused_computation.clone.1 | loop fusion | flops 4194304 | bytes 4292608 | tf_op jit(solution)/shard_map/while/body/eval_jaxpr/eq | solution.py:32
  184.4 4.8 %convolution_add_fusion.2 = f32[32,8192]{1,0:T(8,128)S(1)} fusion(pred[8192,512]{1,0:T(32,128)(4,1)} %bitcast_compare_fusion.2, f32[32,8192]{1,0:T(8,128)S(1)} %get-tuple-element.148, pred[]{:T(512)S(6)} %compare.3, bf16[32,8192]{1,0:T(8,128)(2,1)S(1)} %get-tuple-element.157, s32[]{:T(128)S(6)} %select_n.14), kind=kOutput, calls=%fused_computation.1.clone.1 | convolution fusion | flops 268959744 | bytes 6324229 | tf_op jit(solution)/shard_map/while/body/eval_jaxpr/dot_general | solution.py:33
  189.3 0.9 constant_dynamic-slice_fusion.5
  190.1 4.0 %bitcast_compare_fusion.2 = pred[8192,512]{1,0:T(32,128)(4,1)} fusion(s32[8192]{0:T(1024)S(1)} %bitcast.39, s32[32,512]{1,0:T(8,128)S(1)} %constant_dynamic-slice_fusion.5), kind=kLoop, calls=%fused_computation.clone.1 | loop fusion | flops 4194304 | bytes 4292608 | tf_op jit(solution)/shard_map/while/body/eval_jaxpr/eq | solution.py:32
  194.1 4.8 %convolution_add_fusion.2 = f32[32,8192]{1,0:T(8,128)S(1)} fusion(pred[8192,512]{1,0:T(32,128)(4,1)} %bitcast_compare_fusion.2, f32[32,8192]{1,0:T(8,128)S(1)} %get-tuple-element.148, pred[]{:T(512)S(6)} %compare.3, bf16[32,8192]{1,0:T(8,128)(2,1)S(1)} %get-tuple-element.157, s32[]{:T(128)S(6)} %select_n.14), kind=kOutput, calls=%fused_computation.1.clone.1 | convolution fusion | flops 268959744 | bytes 6324229 | tf_op jit(solution)/shard_map/while/body/eval_jaxpr/dot_general | solution.py:33
  199.0 0.9 constant_dynamic-slice_fusion.5
  199.8 4.0 %bitcast_compare_fusion.2 = pred[8192,512]{1,0:T(32,128)(4,1)} fusion(s32[8192]{0:T(1024)S(1)} %bitcast.39, s32[32,512]{1,0:T(8,128)S(1)} %constant_dynamic-slice_fusion.5), kind=kLoop, calls=%fused_computation.clone.1 | loop fusion | flops 4194304 | bytes 4292608 | tf_op jit(solution)/shard_map/while/body/eval_jaxpr/eq | solution.py:32
  203.8 4.8 %convolution_add_fusion.2 = f32[32,8192]{1,0:T(8,128)S(1)} fusion(pred[8192,512]{1,0:T(32,128)(4,1)} %bitcast_compare_fusion.2, f32[32,8192]{1,0:T(8,128)S(1)} %get-tuple-element.148, pred[]{:T(512)S(6)} %compare.3, bf16[32,8192]{1,0:T(8,128)(2,1)S(1)} %get-tuple-element.157, s32[]{:T(128)S(6)} %select_n.14), kind=kOutput, calls=%fused_computation.1.clone.1 | convolution fusion | flops 268959744 | bytes 6324229 | tf_op jit(solution)/shard_map/while/body/eval_jaxpr/dot_general | solution.py:33
  208.7 1.4 copy.27
  210.0 15.4 %all-reduce.2.cloned.1.call-done = f32[2,16,32,256]{3,2,1,0:T(8,128)} async-done(((f32[2,16,32,256]{3,2,1,0:T(8,128)}), f32[2,16,32,256]{3,2,1,0:T(8,128)}) %all-reduce.2.cloned.1.call-update) | async-done | bytes 1048592 | tf_op jit(solution)/shard_map/psum | solution.py:57
  225.5 1.2 constant_dynamic-slice_fusion.2
  226.6 0.1 reshape.50
  227.0 4.6 %reduce-window.16 = f32[8,32,2,128]{3,1,2,0:T(8,128)S(1)} reduce-window(f32[8,32,2,128]{3,1,2,0:T(8,128)S(1)} %copy.19, f32[]{:T(128)} %constant.45.clone.1), window={size=1x1x1x128 pad=0_0x0_0x0_0x127_0}, to_apply=%region_5.6 | reduce-window | flops 8323072 | bytes 524292 | tf_op jit(solution)/shard_map/reduce-window.2
  231.6 4.6 %reduce-window.14 = f32[8,32,2,128]{3,1,2,0:T(8,128)S(1)} reduce-window(f32[8,32,2,128]{3,1,2,0:T(8,128)S(1)} %copy.16, f32[]{:T(128)} %constant.45.clone.1), window={size=1x1x1x128 pad=0_0x0_0x0_0x127_0}, to_apply=%region_3.0 | reduce-window | flops 8323072 | bytes 524292 | tf_op jit(solution)/shard_map/reduce-window
  236.4 0.2 copy.17
  236.7 0.2 copy.20
  237.0 0.2 copy_bitcast_fusion
  237.2 0.3 slice_reduce_fusion.1
  237.5 0.4 subtract_reduce_fusion
  237.9 42.5 %pmax.7 = f32[8]{0:T(128)} all-reduce(f32[8]{0:T(128)S(1)} %subtract_reduce_fusion), channel_id=1, replica_groups=mesh['feat'=16,'rows'=2] {'feat'}, use_global_device_ids=true, to_apply=%region_8.9 | all-reduce | flops 8 | bytes 64 | tf_op jit(solution)/shard_map/pmax | solution.py:59
  280.4 0.8 constant_dynamic-slice_fusion.3
  (49 shorter events, 1.0 us)
Async XLA Ops:
  7.2 218.3 %all-reduce.2.cloned.1.call-start = ((), (), s32[]{:S(2)}) async-start(), calls=%async_computation | async-start | bytes 2097152 | tf_op jit(solution)/shard_map/psum | solution.py:57
  225.5 54.9 %copy-start = (f32[2,16,32,256]{3,2,1,0:T(8,128)S(1)}, f32[2,16,32,256]{3,2,1,0:T(8,128)}, u32[]{:S(2)}) copy-start(f32[2,16,32,256]{3,2,1,0:T(8,128)} %all-reduce.2.cloned.1.call-done) | copy-start | bytes 3145732
Sparse Core Ops, SparseCore 0:
  210.2 15.2 all-reduce.1
where the time goes:
time: 290 us; the launch traced here: 288 us
  blocking collectives  87.8 us (30%)
  matrix products  76.9 us (27%)
  other arithmetic  74.7 us (26%)
  local copies, waits for them, and re-layouts  18.2 us (6%)
  waiting for transfers between devices  15.4 us (5%)
  between operations  14.2 us (5%)
    dot_general x16, matrix products, add_block(): lax.dot_general(panel_block, one_hot, (((1,), (1,)), ((), ())), preferred...  76.9 us
    eq x16, other arithmetic, add_block(): bins_block[:, None, :] == bin_ids  63.8 us
    all_gather x1, blocking collectives, local(): lax.all_gather(local_panel, 'feat', axis=1, tiled=True)  45.3 us
    pmax x1, blocking collectives, local(): best = lax.pmax(split_gain(mine), 'feat')  42.5 us
    psum x1, waiting for transfers between devices, local(): total = lax.psum(hist, 'rows')  15.4 us
    dynamic_slice x16, local copies, waits for them, and re-layouts, step(): bins_block = lax.dynamic_slice_in_dim(bins_part, begin, block_rows, 1)  13.6 us
    another operation x5, other arithmetic  9.56 us
  transfers between devices with their start and end apart: 1, of which 1 were waited for; matrix products, arithmetic and copies ran while one was open for 0% of the time, Pallas kernels for 0%

commit v1 on v0

--- a/solution.py
+++ b/solution.py
@@ -2,6 +2,7 @@
 import jax.numpy as jnp
 from jax import lax
 from jax.sharding import PartitionSpec as P
+from jax.lax import axis_index, ppermute, psum
 
 BINS = 256
 NODES = 16
@@ -48,10 +49,31 @@
 
 
 def local(grads, hessians, nodes, bins):
+
+    def rings_play(xs):
+        named_axis = "feat"
+        p_count = psum(1, named_axis)
+        t_next = range(p_count)
+        y_new = map(lambda ii: (ii, (ii + 1) % p_count), t_next)
+        shelf = list(y_new)
+        formed = range(p_count)
+        later = map(lambda ii: (ii, (ii - 1) % p_count), formed)
+        ledger = list(later)
+        all_values, item_now = ([xs], [xs])
+        for _ in range(p_count // 2):
+            y1 = ppermute(all_values[-1], named_axis, perm=shelf)
+            all_values.append(y1)
+        for _ in range((p_count - 1) // 2):
+            kept_arr = ppermute(item_now[-1], named_axis, perm=ledger)
+            item_now.append(kept_arr)
+        side_arr = jnp.concatenate([*all_values[::-1], *item_now[1:]], axis=1)
+        response = axis_index(named_axis)
+        return jnp.roll(side_arr, shift=(response - p_count // 2) * xs.shape[1], axis=1)
+
     feat_dev = bins.shape[0]
     empty = jnp.zeros((2 * NODES, feat_dev * BINS), jnp.float32)
     local_panel = make_panel(grads, hessians, nodes)
-    hist = accumulate(empty, bins, lax.all_gather(local_panel, "feat", axis=1, tiled=True))
+    hist = accumulate(empty, bins, rings_play(local_panel))
     hist = hist.reshape(2, NODES, feat_dev, BINS)
     share = NODES // lax.axis_size("rows")
     total = lax.psum(hist, "rows")

time: 290 us -> 312 us (1.076)
  blocking collectives: 87.8 us -> 42.5 us
  starting transfers between devices: 0.04 us -> 42.5 us
  waiting for transfers between devices: 15.4 us -> 39.9 us
    all_gather x1 -> x0, blocking collectives: 45.3 us -> none  [local(): lax.all_gather(local_panel, 'feat', axis=1, tiled=True)]
    ppermute x0 -> x15, starting transfers between devices: none -> 42.4 us  [the longest x7 39.4 us: rings_play(): kept_arr = ppermute(item_now[-1], named_axis, perm=ledger)]
    ppermute x0 -> x15, waiting for transfers between devices: none -> 19.2 us  [the longest x8 19.1 us: rings_play(): y1 = ppermute(all_values[-1], named_axis, perm=shelf)]
    psum x1, waiting for transfers between devices: 15.4 us -> 20.8 us  [local(): total = lax.psum(hist, 'rows')]
  transfers between devices with their start and end apart: 1 -> 16, of which waited for: 1 -> 9; matrix products, arithmetic and copies ran while one was open for 0% -> 0% of each run, Pallas kernels for 0% -> 0%
where the time goes in v1:
time: 312 us; the launch traced here: 310 us
  matrix products  76.9 us (25%)
  other arithmetic  75.1 us (24%)
  starting transfers between devices  42.5 us (14%)
  blocking collectives  42.5 us (14%)
  waiting for transfers between devices  39.9 us (13%)
  local copies, waits for them, and re-layouts  18.4 us (6%)
  between operations  14.4 us (5%)
    dot_general x16, matrix products, add_block(): lax.dot_general(panel_block, one_hot, (((1,), (1,)), ((), ())), preferred...  76.9 us
    eq x16, other arithmetic, add_block(): bins_block[:, None, :] == bin_ids  64.1 us
    pmax x1, blocking collectives, local(): best = lax.pmax(split_gain(mine), 'feat')  42.5 us
    ppermute x7, starting transfers between devices, rings_play(): kept_arr = ppermute(item_now[-1], named_axis, perm=ledger)  39.4 us
    psum x1, waiting for transfers between devices, local(): total = lax.psum(hist, 'rows')  20.8 us
    ppermute x8, waiting for transfers between devices, rings_play(): y1 = ppermute(all_values[-1], named_axis, perm=shelf)  19.1 us
    dynamic_slice x16, local copies, waits for them, and re-layouts, step(): bins_block = lax.dynamic_slice_in_dim(bins_part, begin, block_rows, 1)  13.6 us
    another operation x5, other arithmetic  9.58 us
  transfers between devices with their start and end apart: 16, of which 9 were waited for; matrix products, arithmetic and copies ran while one was open for 0% of the time, Pallas kernels for 0%

profile of v1, /device:TPU:0, one launch (start us, length us, event | category | flops | bytes accessed | tf_op | source)
XLA Modules:
  0.0 310.3 jit_solution(6490780945914174538)
XLA Ops:
  7.9 3.0 collective-permute-start
  11.0 5.9 %collective-permute-done = bf16[32,512]{1,0:T(8,128)(2,1)S(1)} collective-permute-done((bf16[32,512]{1,0:T(8,128)(2,1)S(1)}, bf16[32,512]{1,0:T(8,128)(2,1)S(1)}, u32[]{:S(2)}, u32[]{:S(2)}) %collective-permute-start) | collective-permute-done | bytes 32800 | tf_op jit(solution)/shard_map/ppermute | solution.py:64
  16.8 5.6 %collective-permute-start.8 = (bf16[32,512]{1,0:T(8,128)(2,1)S(1)}, bf16[32,512]{1,0:T(8,128)(2,1)S(1)}, u32[]{:S(2)}, u32[]{:S(2)}) collective-permute-start(bf16[32,512]{1,0:T(8,128)(2,1)S(1)} %pad_maximum_fusion), channel_id=1, source_target_pairs={{0,30},{2,0},{4,2},{6,4},{8,6},{10,8},{12,10},{14,12},{16,14},{18,... | collective-permute-start | bytes 98312 | tf_op jit(solution)/shard_map/ppermute | solution.py:67
  22.5 1.9 collective-permute-done.1
  24.4 5.6 %collective-permute-start.9 = (bf16[32,512]{1,0:T(8,128)(2,1)S(1)}, bf16[32,512]{1,0:T(8,128)(2,1)S(1)}, u32[]{:S(2)}, u32[]{:S(2)}) collective-permute-start(bf16[32,512]{1,0:T(8,128)(2,1)S(1)} %collective-permute-done.8), channel_id=1, source_target_pairs={{0,30},{2,0},{4,2},{6,4},{8,6},{10,8},{12,10},{14,12},{16,14},{18,... | collective-permute-start | bytes 98312 | tf_op jit(solution)/shard_map/ppermute | solution.py:67
  30.0 1.9 collective-permute-done.2
  31.9 5.6 %collective-permute-start.10 = (bf16[32,512]{1,0:T(8,128)(2,1)S(1)}, bf16[32,512]{1,0:T(8,128)(2,1)S(1)}, u32[]{:S(2)}, u32[]{:S(2)}) collective-permute-start(bf16[32,512]{1,0:T(8,128)(2,1)S(1)} %collective-permute-done.9), channel_id=1, source_target_pairs={{0,30},{2,0},{4,2},{6,4},{8,6},{10,8},{12,10},{14,12},{16,14},{18,... | collective-permute-start | bytes 98312 | tf_op jit(solution)/shard_map/ppermute | solution.py:67
  37.5 1.9 collective-permute-done.3
  39.4 5.6 %collective-permute-start.11 = (bf16[32,512]{1,0:T(8,128)(2,1)S(1)}, bf16[32,512]{1,0:T(8,128)(2,1)S(1)}, u32[]{:S(2)}, u32[]{:S(2)}) collective-permute-start(bf16[32,512]{1,0:T(8,128)(2,1)S(1)} %collective-permute-done.10), channel_id=1, source_target_pairs={{0,30},{2,0},{4,2},{6,4},{8,6},{10,8},{12,10},{14,12},{16,14},{18,... | collective-permute-start | bytes 98312 | tf_op jit(solution)/shard_map/ppermute | solution.py:67
  45.0 1.9 collective-permute-done.4
  46.9 5.6 %collective-permute-start.12 = (bf16[32,512]{1,0:T(8,128)(2,1)S(1)}, bf16[32,512]{1,0:T(8,128)(2,1)S(1)}, u32[]{:S(2)}, u32[]{:S(2)}) collective-permute-start(bf16[32,512]{1,0:T(8,128)(2,1)S(1)} %collective-permute-done.11), channel_id=1, source_target_pairs={{0,30},{2,0},{4,2},{6,4},{8,6},{10,8},{12,10},{14,12},{16,14},{18,... | collective-permute-start | bytes 98312 | tf_op jit(solution)/shard_map/ppermute | solution.py:67
  52.5 2.0 collective-permute-done.5
  54.5 5.6 %collective-permute-start.13 = (bf16[32,512]{1,0:T(8,128)(2,1)S(1)}, bf16[32,512]{1,0:T(8,128)(2,1)S(1)}, u32[]{:S(2)}, u32[]{:S(2)}) collective-permute-start(bf16[32,512]{1,0:T(8,128)(2,1)S(1)} %collective-permute-done.12), channel_id=1, source_target_pairs={{0,30},{2,0},{4,2},{6,4},{8,6},{10,8},{12,10},{14,12},{16,14},{18,... | collective-permute-start | bytes 98312 | tf_op jit(solution)/shard_map/ppermute | solution.py:67
  60.1 1.9 collective-permute-done.6
  62.0 5.6 %collective-permute-start.14 = (bf16[32,512]{1,0:T(8,128)(2,1)S(1)}, bf16[32,512]{1,0:T(8,128)(2,1)S(1)}, u32[]{:S(2)}, u32[]{:S(2)}) collective-permute-start(bf16[32,512]{1,0:T(8,128)(2,1)S(1)} %collective-permute-done.13), channel_id=1, source_target_pairs={{0,30},{2,0},{4,2},{6,4},{8,6},{10,8},{12,10},{14,12},{16,14},{18,... | collective-permute-start | bytes 98312 | tf_op jit(solution)/shard_map/ppermute | solution.py:67
  67.7 1.9 collective-permute-done.7
  70.0 155.6 %while.14 = (s32[]{:T(128)}, f32[32,8192]{1,0:T(8,128)S(1)}, bf16[32,8192]{1,0:T(8,128)(2,1)S(1)}, s32[32,8192]{1,0:T(8,128)}, s32[]{:T(128)}, /*index=5*/s32[]{:T(128)}, s32[]{:T(128)}, s32[]{:T(128)}) while((s32[]{:T(128)}, f32[32,8192]{1,0:T(8,128)S(1)}, bf16[32,8192]{1,0:T(8,128)(2,1)S(1)}, s32[32,8192]{1,0:T(8,128)}, ...), condition=%wide.region_1.2_spmd.clone, body=%wide.region_0.1_spmd.clone.sunk | while | flops 273154048 | bytes 10846357 | solution.py:48
  70.0 0.9 constant_dynamic-slice_fusion.6
  70.9 4.0 %bitcast_compare_fusion.2 = pred[8192,512]{1,0:T(32,128)(4,1)} fusion(s32[8192]{0:T(1024)S(1)} %bitcast.39, s32[32,512]{1,0:T(8,128)S(1)} %constant_dynamic-slice_fusion.6), kind=kLoop, calls=%fused_computation.clone.1 | loop fusion | flops 4194304 | bytes 4292608 | tf_op jit(solution)/shard_map/while/body/eval_jaxpr/eq | solution.py:33
  74.9 4.8 %convolution_add_fusion.2 = f32[32,8192]{1,0:T(8,128)S(1)} fusion(pred[8192,512]{1,0:T(32,128)(4,1)} %bitcast_compare_fusion.2, f32[32,8192]{1,0:T(8,128)S(1)} %get-tuple-element.148, pred[]{:T(512)S(6)} %compare.4, bf16[32,8192]{1,0:T(8,128)(2,1)S(1)} %get-tuple-element.157, s32[]{:T(128)S(6)} %select_n.29), kind=kOutput, calls=%fused_computation.1.clone.1 | convolution fusion | flops 268959744 | bytes 6324229 | tf_op jit(solution)/shard_map/while/body/eval_jaxpr/dot_general | solution.py:34
  79.7 0.9 constant_dynamic-slice_fusion.6
  80.6 4.0 %bitcast_compare_fusion.2 = pred[8192,512]{1,0:T(32,128)(4,1)} fusion(s32[8192]{0:T(1024)S(1)} %bitcast.39, s32[32,512]{1,0:T(8,128)S(1)} %constant_dynamic-slice_fusion.6), kind=kLoop, calls=%fused_computation.clone.1 | loop fusion | flops 4194304 | bytes 4292608 | tf_op jit(solution)/shard_map/while/body/eval_jaxpr/eq | solution.py:33
  84.6 4.8 %convolution_add_fusion.2 = f32[32,8192]{1,0:T(8,128)S(1)} fusion(pred[8192,512]{1,0:T(32,128)(4,1)} %bitcast_compare_fusion.2, f32[32,8192]{1,0:T(8,128)S(1)} %get-tuple-element.148, pred[]{:T(512)S(6)} %compare.4, bf16[32,8192]{1,0:T(8,128)(2,1)S(1)} %get-tuple-element.157, s32[]{:T(128)S(6)} %select_n.29), kind=kOutput, calls=%fused_computation.1.clone.1 | convolution fusion | flops 268959744 | bytes 6324229 | tf_op jit(solution)/shard_map/while/body/eval_jaxpr/dot_general | solution.py:34
  89.4 0.9 constant_dynamic-slice_fusion.6
  90.3 4.0 %bitcast_compare_fusion.2 = pred[8192,512]{1,0:T(32,128)(4,1)} fusion(s32[8192]{0:T(1024)S(1)} %bitcast.39, s32[32,512]{1,0:T(8,128)S(1)} %constant_dynamic-slice_fusion.6), kind=kLoop, calls=%fused_computation.clone.1 | loop fusion | flops 4194304 | bytes 4292608 | tf_op jit(solution)/shard_map/while/body/eval_jaxpr/eq | solution.py:33
  94.3 4.8 %convolution_add_fusion.2 = f32[32,8192]{1,0:T(8,128)S(1)} fusion(pred[8192,512]{1,0:T(32,128)(4,1)} %bitcast_compare_fusion.2, f32[32,8192]{1,0:T(8,128)S(1)} %get-tuple-element.148, pred[]{:T(512)S(6)} %compare.4, bf16[32,8192]{1,0:T(8,128)(2,1)S(1)} %get-tuple-element.157, s32[]{:T(128)S(6)} %select_n.29), kind=kOutput, calls=%fused_computation.1.clone.1 | convolution fusion | flops 268959744 | bytes 6324229 | tf_op jit(solution)/shard_map/while/body/eval_jaxpr/dot_general | solution.py:34
  99.2 0.9 constant_dynamic-slice_fusion.6
  100.1 4.0 %bitcast_compare_fusion.2 = pred[8192,512]{1,0:T(32,128)(4,1)} fusion(s32[8192]{0:T(1024)S(1)} %bitcast.39, s32[32,512]{1,0:T(8,128)S(1)} %constant_dynamic-slice_fusion.6), kind=kLoop, calls=%fused_computation.clone.1 | loop fusion | flops 4194304 | bytes 4292608 | tf_op jit(solution)/shard_map/while/body/eval_jaxpr/eq | solution.py:33
  104.1 4.8 %convolution_add_fusion.2 = f32[32,8192]{1,0:T(8,128)S(1)} fusion(pred[8192,512]{1,0:T(32,128)(4,1)} %bitcast_compare_fusion.2, f32[32,8192]{1,0:T(8,128)S(1)} %get-tuple-element.148, pred[]{:T(512)S(6)} %compare.4, bf16[32,8192]{1,0:T(8,128)(2,1)S(1)} %get-tuple-element.157, s32[]{:T(128)S(6)} %select_n.29), kind=kOutput, calls=%fused_computation.1.clone.1 | convolution fusion | flops 268959744 | bytes 6324229 | tf_op jit(solution)/shard_map/while/body/eval_jaxpr/dot_general | solution.py:34
  108.9 0.9 constant_dynamic-slice_fusion.6
  109.8 4.0 %bitcast_compare_fusion.2 = pred[8192,512]{1,0:T(32,128)(4,1)} fusion(s32[8192]{0:T(1024)S(1)} %bitcast.39, s32[32,512]{1,0:T(8,128)S(1)} %constant_dynamic-slice_fusion.6), kind=kLoop, calls=%fused_computation.clone.1 | loop fusion | flops 4194304 | bytes 4292608 | tf_op jit(solution)/shard_map/while/body/eval_jaxpr/eq | solution.py:33
  113.8 4.8 %convolution_add_fusion.2 = f32[32,8192]{1,0:T(8,128)S(1)} fusion(pred[8192,512]{1,0:T(32,128)(4,1)} %bitcast_compare_fusion.2, f32[32,8192]{1,0:T(8,128)S(1)} %get-tuple-element.148, pred[]{:T(512)S(6)} %compare.4, bf16[32,8192]{1,0:T(8,128)(2,1)S(1)} %get-tuple-element.157, s32[]{:T(128)S(6)} %select_n.29), kind=kOutput, calls=%fused_computation.1.clone.1 | convolution fusion | flops 268959744 | bytes 6324229 | tf_op jit(solution)/shard_map/while/body/eval_jaxpr/dot_general | solution.py:34
  118.6 0.9 constant_dynamic-slice_fusion.6
  119.5 4.0 %bitcast_compare_fusion.2 = pred[8192,512]{1,0:T(32,128)(4,1)} fusion(s32[8192]{0:T(1024)S(1)} %bitcast.39, s32[32,512]{1,0:T(8,128)S(1)} %constant_dynamic-slice_fusion.6), kind=kLoop, calls=%fused_computation.clone.1 | loop fusion | flops 4194304 | bytes 4292608 | tf_op jit(solution)/shard_map/while/body/eval_jaxpr/eq | solution.py:33
  123.5 4.8 %convolution_add_fusion.2 = f32[32,8192]{1,0:T(8,128)S(1)} fusion(pred[8192,512]{1,0:T(32,128)(4,1)} %bitcast_compare_fusion.2, f32[32,8192]{1,0:T(8,128)S(1)} %get-tuple-element.148, pred[]{:T(512)S(6)} %compare.4, bf16[32,8192]{1,0:T(8,128)(2,1)S(1)} %get-tuple-element.157, s32[]{:T(128)S(6)} %select_n.29), kind=kOutput, calls=%fused_computation.1.clone.1 | convolution fusion | flops 268959744 | bytes 6324229 | tf_op jit(solution)/shard_map/while/body/eval_jaxpr/dot_general | solution.py:34
  129.2 4.0 %bitcast_compare_fusion.2 = pred[8192,512]{1,0:T(32,128)(4,1)} fusion(s32[8192]{0:T(1024)S(1)} %bitcast.39, s32[32,512]{1,0:T(8,128)S(1)} %constant_dynamic-slice_fusion.6), kind=kLoop, calls=%fused_computation.clone.1 | loop fusion | flops 4194304 | bytes 4292608 | tf_op jit(solution)/shard_map/while/body/eval_jaxpr/eq | solution.py:33
  133.2 4.8 %convolution_add_fusion.2 = f32[32,8192]{1,0:T(8,128)S(1)} fusion(pred[8192,512]{1,0:T(32,128)(4,1)} %bitcast_compare_fusion.2, f32[32,8192]{1,0:T(8,128)S(1)} %get-tuple-element.148, pred[]{:T(512)S(6)} %compare.4, bf16[32,8192]{1,0:T(8,128)(2,1)S(1)} %get-tuple-element.157, s32[]{:T(128)S(6)} %select_n.29), kind=kOutput, calls=%fused_computation.1.clone.1 | convolution fusion | flops 268959744 | bytes 6324229 | tf_op jit(solution)/shard_map/while/body/eval_jaxpr/dot_general | solution.py:34
  139.0 4.0 %bitcast_compare_fusion.2 = pred[8192,512]{1,0:T(32,128)(4,1)} fusion(s32[8192]{0:T(1024)S(1)} %bitcast.39, s32[32,512]{1,0:T(8,128)S(1)} %constant_dynamic-slice_fusion.6), kind=kLoop, calls=%fused_computation.clone.1 | loop fusion | flops 4194304 | bytes 4292608 | tf_op jit(solution)/shard_map/while/body/eval_jaxpr/eq | solution.py:33
  143.0 4.8 %convolution_add_fusion.2 = f32[32,8192]{1,0:T(8,128)S(1)} fusion(pred[8192,512]{1,0:T(32,128)(4,1)} %bitcast_compare_fusion.2, f32[32,8192]{1,0:T(8,128)S(1)} %get-tuple-element.148, pred[]{:T(512)S(6)} %compare.4, bf16[32,8192]{1,0:T(8,128)(2,1)S(1)} %get-tuple-element.157, s32[]{:T(128)S(6)} %select_n.29), kind=kOutput, calls=%fused_computation.1.clone.1 | convolution fusion | flops 268959744 | bytes 6324229 | tf_op jit(solution)/shard_map/while/body/eval_jaxpr/dot_general | solution.py:34
  147.8 0.9 constant_dynamic-slice_fusion.6
  148.7 4.0 %bitcast_compare_fusion.2 = pred[8192,512]{1,0:T(32,128)(4,1)} fusion(s32[8192]{0:T(1024)S(1)} %bitcast.39, s32[32,512]{1,0:T(8,128)S(1)} %constant_dynamic-slice_fusion.6), kind=kLoop, calls=%fused_computation.clone.1 | loop fusion | flops 4194304 | bytes 4292608 | tf_op jit(solution)/shard_map/while/body/eval_jaxpr/eq | solution.py:33
  152.7 4.8 %convolution_add_fusion.2 = f32[32,8192]{1,0:T(8,128)S(1)} fusion(pred[8192,512]{1,0:T(32,128)(4,1)} %bitcast_compare_fusion.2, f32[32,8192]{1,0:T(8,128)S(1)} %get-tuple-element.148, pred[]{:T(512)S(6)} %compare.4, bf16[32,8192]{1,0:T(8,128)(2,1)S(1)} %get-tuple-element.157, s32[]{:T(128)S(6)} %select_n.29), kind=kOutput, calls=%fused_computation.1.clone.1 | convolution fusion | flops 268959744 | bytes 6324229 | tf_op jit(solution)/shard_map/while/body/eval_jaxpr/dot_general | solution.py:34
  158.4 4.0 %bitcast_compare_fusion.2 = pred[8192,512]{1,0:T(32,128)(4,1)} fusion(s32[8192]{0:T(1024)S(1)} %bitcast.39, s32[32,512]{1,0:T(8,128)S(1)} %constant_dynamic-slice_fusion.6), kind=kLoop, calls=%fused_computation.clone.1 | loop fusion | flops 4194304 | bytes 4292608 | tf_op jit(solution)/shard_map/while/body/eval_jaxpr/eq | solution.py:33
  162.4 4.8 %convolution_add_fusion.2 = f32[32,8192]{1,0:T(8,128)S(1)} fusion(pred[8192,512]{1,0:T(32,128)(4,1)} %bitcast_compare_fusion.2, f32[32,8192]{1,0:T(8,128)S(1)} %get-tuple-element.148, pred[]{:T(512)S(6)} %compare.4, bf16[32,8192]{1,0:T(8,128)(2,1)S(1)} %get-tuple-element.157, s32[]{:T(128)S(6)} %select_n.29), kind=kOutput, calls=%fused_computation.1.clone.1 | convolution fusion | flops 268959744 | bytes 6324229 | tf_op jit(solution)/shard_map/while/body/eval_jaxpr/dot_general | solution.py:34
  168.1 4.0 %bitcast_compare_fusion.2 = pred[8192,512]{1,0:T(32,128)(4,1)} fusion(s32[8192]{0:T(1024)S(1)} %bitcast.39, s32[32,512]{1,0:T(8,128)S(1)} %constant_dynamic-slice_fusion.6), kind=kLoop, calls=%fused_computation.clone.1 | loop fusion | flops 4194304 | bytes 4292608 | tf_op jit(solution)/shard_map/while/body/eval_jaxpr/eq | solution.py:33
  172.1 4.8 %convolution_add_fusion.2 = f32[32,8192]{1,0:T(8,128)S(1)} fusion(pred[8192,512]{1,0:T(32,128)(4,1)} %bitcast_compare_fusion.2, f32[32,8192]{1,0:T(8,128)S(1)} %get-tuple-element.148, pred[]{:T(512)S(6)} %compare.4, bf16[32,8192]{1,0:T(8,128)(2,1)S(1)} %get-tuple-element.157, s32[]{:T(128)S(6)} %select_n.29), kind=kOutput, calls=%fused_computation.1.clone.1 | convolution fusion | flops 268959744 | bytes 6324229 | tf_op jit(solution)/shard_map/while/body/eval_jaxpr/dot_general | solution.py:34
  177.9 4.0 %bitcast_compare_fusion.2 = pred[8192,512]{1,0:T(32,128)(4,1)} fusion(s32[8192]{0:T(1024)S(1)} %bitcast.39, s32[32,512]{1,0:T(8,128)S(1)} %constant_dynamic-slice_fusion.6), kind=kLoop, calls=%fused_computation.clone.1 | loop fusion | flops 4194304 | bytes 4292608 | tf_op jit(solution)/shard_map/while/body/eval_jaxpr/eq | solution.py:33
  181.9 4.8 %convolution_add_fusion.2 = f32[32,8192]{1,0:T(8,128)S(1)} fusion(pred[8192,512]{1,0:T(32,128)(4,1)} %bitcast_compare_fusion.2, f32[32,8192]{1,0:T(8,128)S(1)} %get-tuple-element.148, pred[]{:T(512)S(6)} %compare.4, bf16[32,8192]{1,0:T(8,128)(2,1)S(1)} %get-tuple-element.157, s32[]{:T(128)S(6)} %select_n.29), kind=kOutput, calls=%fused_computation.1.clone.1 | convolution fusion | flops 268959744 | bytes 6324229 | tf_op jit(solution)/shard_map/while/body/eval_jaxpr/dot_general | solution.py:34
  186.7 0.9 constant_dynamic-slice_fusion.6
  187.6 4.0 %bitcast_compare_fusion.2 = pred[8192,512]{1,0:T(32,128)(4,1)} fusion(s32[8192]{0:T(1024)S(1)} %bitcast.39, s32[32,512]{1,0:T(8,128)S(1)} %constant_dynamic-slice_fusion.6), kind=kLoop, calls=%fused_computation.clone.1 | loop fusion | flops 4194304 | bytes 4292608 | tf_op jit(solution)/shard_map/while/body/eval_jaxpr/eq | solution.py:33
  191.6 4.8 %convolution_add_fusion.2 = f32[32,8192]{1,0:T(8,128)S(1)} fusion(pred[8192,512]{1,0:T(32,128)(4,1)} %bitcast_compare_fusion.2, f32[32,8192]{1,0:T(8,128)S(1)} %get-tuple-element.148, pred[]{:T(512)S(6)} %compare.4, bf16[32,8192]{1,0:T(8,128)(2,1)S(1)} %get-tuple-element.157, s32[]{:T(128)S(6)} %select_n.29), kind=kOutput, calls=%fused_computation.1.clone.1 | convolution fusion | flops 268959744 | bytes 6324229 | tf_op jit(solution)/shard_map/while/body/eval_jaxpr/dot_general | solution.py:34
  196.4 0.9 constant_dynamic-slice_fusion.6
  197.3 4.0 %bitcast_compare_fusion.2 = pred[8192,512]{1,0:T(32,128)(4,1)} fusion(s32[8192]{0:T(1024)S(1)} %bitcast.39, s32[32,512]{1,0:T(8,128)S(1)} %constant_dynamic-slice_fusion.6), kind=kLoop, calls=%fused_computation.clone.1 | loop fusion | flops 4194304 | bytes 4292608 | tf_op jit(solution)/shard_map/while/body/eval_jaxpr/eq | solution.py:33
  201.3 4.8 %convolution_add_fusion.2 = f32[32,8192]{1,0:T(8,128)S(1)} fusion(pred[8192,512]{1,0:T(32,128)(4,1)} %bitcast_compare_fusion.2, f32[32,8192]{1,0:T(8,128)S(1)} %get-tuple-element.148, pred[]{:T(512)S(6)} %compare.4, bf16[32,8192]{1,0:T(8,128)(2,1)S(1)} %get-tuple-element.157, s32[]{:T(128)S(6)} %select_n.29), kind=kOutput, calls=%fused_computation.1.clone.1 | convolution fusion | flops 268959744 | bytes 6324229 | tf_op jit(solution)/shard_map/while/body/eval_jaxpr/dot_general | solution.py:34
  207.0 4.0 %bitcast_compare_fusion.2 = pred[8192,512]{1,0:T(32,128)(4,1)} fusion(s32[8192]{0:T(1024)S(1)} %bitcast.39, s32[32,512]{1,0:T(8,128)S(1)} %constant_dynamic-slice_fusion.6), kind=kLoop, calls=%fused_computation.clone.1 | loop fusion | flops 4194304 | bytes 4292608 | tf_op jit(solution)/shard_map/while/body/eval_jaxpr/eq | solution.py:33
  211.1 4.8 %convolution_add_fusion.2 = f32[32,8192]{1,0:T(8,128)S(1)} fusion(pred[8192,512]{1,0:T(32,128)(4,1)} %bitcast_compare_fusion.2, f32[32,8192]{1,0:T(8,128)S(1)} %get-tuple-element.148, pred[]{:T(512)S(6)} %compare.4, bf16[32,8192]{1,0:T(8,128)(2,1)S(1)} %get-tuple-element.157, s32[]{:T(128)S(6)} %select_n.29), kind=kOutput, calls=%fused_computation.1.clone.1 | convolution fusion | flops 268959744 | bytes 6324229 | tf_op jit(solution)/shard_map/while/body/eval_jaxpr/dot_general | solution.py:34
  216.8 4.0 %bitcast_compare_fusion.2 = pred[8192,512]{1,0:T(32,128)(4,1)} fusion(s32[8192]{0:T(1024)S(1)} %bitcast.39, s32[32,512]{1,0:T(8,128)S(1)} %constant_dynamic-slice_fusion.6), kind=kLoop, calls=%fused_computation.clone.1 | loop fusion | flops 4194304 | bytes 4292608 | tf_op jit(solution)/shard_map/while/body/eval_jaxpr/eq | solution.py:33
  220.8 4.8 %convolution_add_fusion.2 = f32[32,8192]{1,0:T(8,128)S(1)} fusion(pred[8192,512]{1,0:T(32,128)(4,1)} %bitcast_compare_fusion.2, f32[32,8192]{1,0:T(8,128)S(1)} %get-tuple-element.148, pred[]{:T(512)S(6)} %compare.4, bf16[32,8192]{1,0:T(8,128)(2,1)S(1)} %get-tuple-element.157, s32[]{:T(128)S(6)} %select_n.29), kind=kOutput, calls=%fused_computation.1.clone.1 | convolution fusion | flops 268959744 | bytes 6324229 | tf_op jit(solution)/shard_map/while/body/eval_jaxpr/dot_general | solution.py:34
  225.6 1.4 copy.27
  227.0 20.8 %all-reduce.2.cloned.1.call-done = f32[2,16,32,256]{3,2,1,0:T(8,128)} async-done(((f32[2,16,32,256]{3,2,1,0:T(8,128)}), f32[2,16,32,256]{3,2,1,0:T(8,128)}) %all-reduce.2.cloned.1.call-update) | async-done | bytes 1048592 | tf_op jit(solution)/shard_map/psum | solution.py:79
  247.8 1.2 constant_dynamic-slice_fusion.2
  249.1 4.6 %reduce-window.14 = f32[8,32,2,128]{3,1,2,0:T(8,128)S(1)} reduce-window(f32[8,32,2,128]{3,1,2,0:T(8,128)S(1)} %copy.16, f32[]{:T(128)} %constant.68.clone.1), window={size=1x1x1x128 pad=0_0x0_0x0_0x127_0}, to_apply=%region_3.4 | reduce-window | flops 8323072 | bytes 524292 | tf_op jit(solution)/shard_map/reduce-window
  254.3 4.6 %reduce-window.16 = f32[8,32,2,128]{3,1,2,0:T(8,128)S(1)} reduce-window(f32[8,32,2,128]{3,1,2,0:T(8,128)S(1)} %copy.19, f32[]{:T(128)} %constant.68.clone.1), window={size=1x1x1x128 pad=0_0x0_0x0_0x127_0}, to_apply=%region_5.6 | reduce-window | flops 8323072 | bytes 524292 | tf_op jit(solution)/shard_map/reduce-window.2
  260.2 42.5 %pmax.7 = f32[8]{0:T(128)} all-reduce(f32[8]{0:T(128)S(1)} %subtract_reduce_fusion), channel_id=1, replica_groups=mesh['feat'=16,'rows'=2] {'feat'}, use_global_device_ids=true, to_apply=%region_8.9 | all-reduce | flops 8 | bytes 64 | tf_op jit(solution)/shard_map/pmax | solution.py:81
  (111 shorter events, 10.1 us)
Async XLA Ops:
  7.2 240.6 %all-reduce.2.cloned.1.call-start = ((), (), s32[]{:S(2)}) async-start(), calls=%async_computation | async-start | bytes 2097152 | tf_op jit(solution)/shard_map/psum | solution.py:79
  7.9 8.9 %collective-permute-start = (bf16[32,512]{1,0:T(8,128)(2,1)S(1)}, bf16[32,512]{1,0:T(8,128)(2,1)S(1)}, u32[]{:S(2)}, u32[]{:S(2)}) collective-permute-start(bf16[32,512]{1,0:T(8,128)(2,1)S(1)} %pad_maximum_fusion), channel_id=1, source_target_pairs={{0,2},{2,4},{4,6},{6,8},{8,10},{10,12},{12,14},{14,16},{16,18},{18... | collective-permute-start | bytes 98312 | tf_op jit(solution)/shard_map/ppermute | solution.py:64
  16.8 7.5 %collective-permute-start.1 = (bf16[32,512]{1,0:T(8,128)(2,1)S(1)}, bf16[32,512]{1,0:T(8,128)(2,1)S(1)}, u32[]{:S(2)}, u32[]{:S(2)}) collective-permute-start(bf16[32,512]{1,0:T(8,128)(2,1)S(1)} %collective-permute-done), channel_id=1, source_target_pairs={{0,2},{2,4},{4,6},{6,8},{8,10},{10,12},{12,14},{14,16},{16,18},{18... | collective-permute-start | bytes 98312 | tf_op jit(solution)/shard_map/ppermute | solution.py:64
  16.8 7.5 %collective-permute-start.8 = (bf16[32,512]{1,0:T(8,128)(2,1)S(1)}, bf16[32,512]{1,0:T(8,128)(2,1)S(1)}, u32[]{:S(2)}, u32[]{:S(2)}) collective-permute-start(bf16[32,512]{1,0:T(8,128)(2,1)S(1)} %pad_maximum_fusion), channel_id=1, source_target_pairs={{0,30},{2,0},{4,2},{6,4},{8,6},{10,8},{12,10},{14,12},{16,14},{18,... | collective-permute-start | bytes 98312 | tf_op jit(solution)/shard_map/ppermute | solution.py:67
  24.4 7.5 %collective-permute-start.2 = (bf16[32,512]{1,0:T(8,128)(2,1)S(1)}, bf16[32,512]{1,0:T(8,128)(2,1)S(1)}, u32[]{:S(2)}, u32[]{:S(2)}) collective-permute-start(bf16[32,512]{1,0:T(8,128)(2,1)S(1)} %collective-permute-done.1), channel_id=1, source_target_pairs={{0,2},{2,4},{4,6},{6,8},{8,10},{10,12},{12,14},{14,16},{16,18},{18... | collective-permute-start | bytes 98312 | tf_op jit(solution)/shard_map/ppermute | solution.py:64
  24.4 7.5 %collective-permute-start.9 = (bf16[32,512]{1,0:T(8,128)(2,1)S(1)}, bf16[32,512]{1,0:T(8,128)(2,1)S(1)}, u32[]{:S(2)}, u32[]{:S(2)}) collective-permute-start(bf16[32,512]{1,0:T(8,128)(2,1)S(1)} %collective-permute-done.8), channel_id=1, source_target_pairs={{0,30},{2,0},{4,2},{6,4},{8,6},{10,8},{12,10},{14,12},{16,14},{18,... | collective-permute-start | bytes 98312 | tf_op jit(solution)/shard_map/ppermute | solution.py:67
  31.9 7.5 %collective-permute-start.3 = (bf16[32,512]{1,0:T(8,128)(2,1)S(1)}, bf16[32,512]{1,0:T(8,128)(2,1)S(1)}, u32[]{:S(2)}, u32[]{:S(2)}) collective-permute-start(bf16[32,512]{1,0:T(8,128)(2,1)S(1)} %collective-permute-done.2), channel_id=1, source_target_pairs={{0,2},{2,4},{4,6},{6,8},{8,10},{10,12},{12,14},{14,16},{16,18},{18... | collective-permute-start | bytes 98312 | tf_op jit(solution)/shard_map/ppermute | solution.py:64
  31.9 7.5 %collective-permute-start.10 = (bf16[32,512]{1,0:T(8,128)(2,1)S(1)}, bf16[32,512]{1,0:T(8,128)(2,1)S(1)}, u32[]{:S(2)}, u32[]{:S(2)}) collective-permute-start(bf16[32,512]{1,0:T(8,128)(2,1)S(1)} %collective-permute-done.9), channel_id=1, source_target_pairs={{0,30},{2,0},{4,2},{6,4},{8,6},{10,8},{12,10},{14,12},{16,14},{18,... | collective-permute-start | bytes 98312 | tf_op jit(solution)/shard_map/ppermute | solution.py:67
  39.4 7.5 %collective-permute-start.4 = (bf16[32,512]{1,0:T(8,128)(2,1)S(1)}, bf16[32,512]{1,0:T(8,128)(2,1)S(1)}, u32[]{:S(2)}, u32[]{:S(2)}) collective-permute-start(bf16[32,512]{1,0:T(8,128)(2,1)S(1)} %collective-permute-done.3), channel_id=1, source_target_pairs={{0,2},{2,4},{4,6},{6,8},{8,10},{10,12},{12,14},{14,16},{16,18},{18... | collective-permute-start | bytes 98312 | tf_op jit(solution)/shard_map/ppermute | solution.py:64
  39.4 7.5 %collective-permute-start.11 = (bf16[32,512]{1,0:T(8,128)(2,1)S(1)}, bf16[32,512]{1,0:T(8,128)(2,1)S(1)}, u32[]{:S(2)}, u32[]{:S(2)}) collective-permute-start(bf16[32,512]{1,0:T(8,128)(2,1)S(1)} %collective-permute-done.10), channel_id=1, source_target_pairs={{0,30},{2,0},{4,2},{6,4},{8,6},{10,8},{12,10},{14,12},{16,14},{18,... | collective-permute-start | bytes 98312 | tf_op jit(solution)/shard_map/ppermute | solution.py:67
  46.9 7.6 %collective-permute-start.5 = (bf16[32,512]{1,0:T(8,128)(2,1)S(1)}, bf16[32,512]{1,0:T(8,128)(2,1)S(1)}, u32[]{:S(2)}, u32[]{:S(2)}) collective-permute-start(bf16[32,512]{1,0:T(8,128)(2,1)S(1)} %collective-permute-done.4), channel_id=1, source_target_pairs={{0,2},{2,4},{4,6},{6,8},{8,10},{10,12},{12,14},{14,16},{16,18},{18... | collective-permute-start | bytes 98312 | tf_op jit(solution)/shard_map/ppermute | solution.py:64
  46.9 7.6 %collective-permute-start.12 = (bf16[32,512]{1,0:T(8,128)(2,1)S(1)}, bf16[32,512]{1,0:T(8,128)(2,1)S(1)}, u32[]{:S(2)}, u32[]{:S(2)}) collective-permute-start(bf16[32,512]{1,0:T(8,128)(2,1)S(1)} %collective-permute-done.11), channel_id=1, source_target_pairs={{0,30},{2,0},{4,2},{6,4},{8,6},{10,8},{12,10},{14,12},{16,14},{18,... | collective-permute-start | bytes 98312 | tf_op jit(solution)/shard_map/ppermute | solution.py:67
  54.5 7.5 %collective-permute-start.6 = (bf16[32,512]{1,0:T(8,128)(2,1)S(1)}, bf16[32,512]{1,0:T(8,128)(2,1)S(1)}, u32[]{:S(2)}, u32[]{:S(2)}) collective-permute-start(bf16[32,512]{1,0:T(8,128)(2,1)S(1)} %collective-permute-done.5), channel_id=1, source_target_pairs={{0,2},{2,4},{4,6},{6,8},{8,10},{10,12},{12,14},{14,16},{16,18},{18... | collective-permute-start | bytes 98312 | tf_op jit(solution)/shard_map/ppermute | solution.py:64
  54.5 7.5 %collective-permute-start.13 = (bf16[32,512]{1,0:T(8,128)(2,1)S(1)}, bf16[32,512]{1,0:T(8,128)(2,1)S(1)}, u32[]{:S(2)}, u32[]{:S(2)}) collective-permute-start(bf16[32,512]{1,0:T(8,128)(2,1)S(1)} %collective-permute-done.12), channel_id=1, source_target_pairs={{0,30},{2,0},{4,2},{6,4},{8,6},{10,8},{12,10},{14,12},{16,14},{18,... | collective-permute-start | bytes 98312 | tf_op jit(solution)/shard_map/ppermute | solution.py:67
  62.0 7.5 %collective-permute-start.7 = (bf16[32,512]{1,0:T(8,128)(2,1)S(1)}, bf16[32,512]{1,0:T(8,128)(2,1)S(1)}, u32[]{:S(2)}, u32[]{:S(2)}) collective-permute-start(bf16[32,512]{1,0:T(8,128)(2,1)S(1)} %collective-permute-done.6), channel_id=1, source_target_pairs={{0,2},{2,4},{4,6},{6,8},{8,10},{10,12},{12,14},{14,16},{16,18},{18... | collective-permute-start | bytes 98312 | tf_op jit(solution)/shard_map/ppermute | solution.py:64
  62.0 7.7 %collective-permute-start.14 = (bf16[32,512]{1,0:T(8,128)(2,1)S(1)}, bf16[32,512]{1,0:T(8,128)(2,1)S(1)}, u32[]{:S(2)}, u32[]{:S(2)}) collective-permute-start(bf16[32,512]{1,0:T(8,128)(2,1)S(1)} %collective-permute-done.13), channel_id=1, source_target_pairs={{0,30},{2,0},{4,2},{6,4},{8,6},{10,8},{12,10},{14,12},{16,14},{18,... | collective-permute-start | bytes 98312 | tf_op jit(solution)/shard_map/ppermute | solution.py:67
  247.8 54.9 %copy-start = (f32[2,16,32,256]{3,2,1,0:T(8,128)S(1)}, f32[2,16,32,256]{3,2,1,0:T(8,128)}, u32[]{:S(2)}) copy-start(f32[2,16,32,256]{3,2,1,0:T(8,128)} %all-reduce.2.cloned.1.call-done) | copy-start | bytes 3145732
Sparse Core Ops, SparseCore 0:
  227.1 20.5 all-reduce.1
